TPU v7x, 32 devices: a whole 2x2x4 slice. The times are simulated.
32 devices in a mesh: dp: 8 (over y, x, core), section: 4 (over z).
Axes of the slice: x: 2, y: 2, z: 4, core: 2. Of those that a mesh axis runs over, the one named last changes fastest.
Arguments:
- inputs: bfloat16 [1280, 8192], P('dp'), may hold values from -6 to 6
- cotangent: bfloat16 [1280, 8192], P('dp'), may hold values from -0.625 to 0.625
- weight_in: bfloat16 [4, 8192, 512], P('section'), may hold values from -0.0625 to 0.0625
- weight_out: bfloat16 [4, 8192, 512], P('section'), may hold values from -0.25 to 0.25
- norm_gains: float32 [4, 8192], P('section'), may hold values from 0.1 to 1.9
Outputs:
- in_grad: float32 [4, 8192, 512], P('section', 'dp')
- out_grad: float32 [4, 8192, 512], P('section', 'dp')
- gain_grad: float32 [4, 8192], P('section', 'dp')
All inputs are finite; a program needn't handle non-finite values.
Results may differ from a plain program's by a relative error of at most 0.025.
Values may be sent and summed in bfloat16 or wider, within the bound.
A program may use at most 192 MiB of HBM per device.

v0:
```python
import jax
import jax.numpy as jnp
from jax import lax
from jax.sharding import PartitionSpec as P

ROWS = 40
MICRO = 4


EPSILON = 1e-05


def from_behind(block, axis, distance):
    devices = range(lax.axis_size(axis))
    route = [(i - distance, i) for i in devices if i - distance in devices]
    return lax.ppermute(block, axis, route)


def from_partner(value, axis, stride):
    mask = 2**stride
    pairs = [(source, source ^ mask) for source in range(lax.axis_size(axis))]
    return lax.ppermute(value, axis, pairs)


def normalize(block_rows, gain_row):
    values = block_rows.astype(jnp.float32)
    row_scale = lax.rsqrt(jnp.mean(values * values, axis=1, keepdims=True) + EPSILON)
    normed = (values * row_scale * gain_row).astype(jnp.bfloat16)
    return (values, row_scale, normed)


def layer_forward(block_rows, w_in, w_out, gain_row):
    values, row_scale, normed = normalize(block_rows, gain_row)
    pre_act = jnp.dot(normed, w_in, preferred_element_type=jnp.float32)
    activated = jax.nn.silu(pre_act).astype(jnp.bfloat16)
    branch = lax.dot_general(
        activated, w_out, (((1,), (1,)), ((), ())), preferred_element_type=jnp.float32
    )
    return (values + branch).astype(jnp.bfloat16)


def backward_parts(block_rows, upstream, w_in, w_out, gain_row):
    values, row_scale, normed = normalize(block_rows, gain_row)
    pre_act = jnp.dot(normed, w_in, preferred_element_type=jnp.float32)
    activated = jax.nn.silu(pre_act).astype(jnp.bfloat16)
    grad_act = jnp.dot(upstream, w_out, preferred_element_type=jnp.float32)
    sigmoid_pre = jax.nn.sigmoid(pre_act)
    grad_pre = (grad_act * sigmoid_pre * (1.0 + pre_act * (1.0 - sigmoid_pre))).astype(jnp.bfloat16)
    grad_norm = lax.dot_general(
        grad_pre, w_in, (((1,), (1,)), ((), ())), preferred_element_type=jnp.float32
    )
    scaled = grad_norm * gain_row
    centered = jnp.mean(scaled * values, axis=1, keepdims=True)
    grad_in = (
        upstream.astype(jnp.float32) + row_scale * scaled - values * row_scale**3 * centered
    ).astype(jnp.bfloat16)
    gain_rows = grad_norm * values * row_scale
    return (grad_in, normed, grad_pre, activated, gain_rows)


def column_product(left, right):
    return lax.dot_general(
        left, right, (((0,), (0,)), ((), ())), preferred_element_type=jnp.float32
    )


def put_slot(stored, fresh, micro_slot, is_live):
    kept_rows = lax.dynamic_index_in_dim(stored, micro_slot, 0, keepdims=False)
    return lax.dynamic_update_index_in_dim(
        stored, jnp.where(is_live, fresh, kept_rows), micro_slot, 0
    )


def send_back(grad_in):
    return from_behind(grad_in, "section", -1)


def move_mirror(block, sections):
    for bit in range(sections.bit_length() - 1):
        block = from_partner(block, "section", bit)
    return block


def local(inputs, cotangent, weight_in, weight_out, norm_gains):
    w_in = weight_in[0]
    w_out = weight_out[0]
    gain_row = norm_gains[0]
    sections = lax.axis_size("section")
    section_pos = lax.axis_index("section")
    model_width = inputs.shape[1]
    hidden_width = w_in.shape[1]
    micro_in = inputs.reshape(MICRO, ROWS, model_width)
    micro_grad = cotangent.reshape(MICRO, ROWS, model_width)
    tick_count = MICRO + sections - 1
    blank_rows = jnp.zeros((ROWS, model_width), jnp.bfloat16)

    def forward_tick(tick_num, carried):
        incoming, stashed = carried
        micro_pos = tick_num - section_pos
        is_live = (micro_pos >= 0) & (micro_pos < MICRO)
        micro_slot = jnp.clip(micro_pos, 0, MICRO - 1)
        first_rows = lax.dynamic_index_in_dim(micro_in, micro_slot, 0, keepdims=False)
        block_in = jnp.where(section_pos == 0, first_rows, incoming)
        stashed = put_slot(stashed, block_in, micro_slot, is_live)
        produced = lax.cond(
            is_live & (section_pos < sections - 1),
            lambda block_rows: layer_forward(block_rows, w_in, w_out, gain_row),
            jnp.zeros_like,
            block_in,
        )
        incoming = from_behind(produced, "section", 1)
        return (incoming, stashed)

    stash_init = jnp.zeros((MICRO, ROWS, model_width), jnp.bfloat16)
    finished, stashed = lax.fori_loop(0, tick_count, forward_tick, (blank_rows, stash_init))

    def live_slot(tick_num):
        micro_pos = tick_num - (sections - 1 - section_pos)
        is_live = (micro_pos >= 0) & (micro_pos < MICRO)
        return (is_live, jnp.clip(micro_pos, 0, MICRO - 1))

    def upstream_of(incoming, micro_slot):
        last_rows = lax.dynamic_index_in_dim(micro_grad, micro_slot, 0, keepdims=False)
        return jnp.where(section_pos == sections - 1, last_rows, incoming)

    def make_tick(stash_view):

        def backward_tick(tick_num, carried):
            incoming, store_norm, store_pre, store_up, store_act, gain_acc = carried
            is_live, micro_slot = live_slot(tick_num)
            upstream = upstream_of(incoming, micro_slot)
            block_rows = lax.dynamic_index_in_dim(stash_view, micro_slot, 0, keepdims=False)

            def compute(operands):
                grad_in, normed, grad_pre, activated, gain_rows = backward_parts(
                    operands[0], operands[1], w_in, w_out, gain_row
                )
                return (grad_in, normed, grad_pre, activated, jnp.sum(gain_rows, axis=0))

            def skip_tick(operands):
                narrow_zero = jnp.zeros((ROWS, hidden_width), jnp.bfloat16)
                return (
                    jnp.zeros_like(operands[0]),
                    jnp.zeros_like(operands[0]),
                    narrow_zero,
                    narrow_zero,
                    jnp.zeros((model_width,), jnp.float32),
                )

            grad_in, normed, grad_pre, activated, gain_sum = lax.cond(
                is_live, compute, skip_tick, (block_rows, upstream)
            )
            store_norm = put_slot(store_norm, normed, micro_slot, is_live)
            store_pre = put_slot(store_pre, grad_pre, micro_slot, is_live)
            store_up = put_slot(store_up, upstream, micro_slot, is_live)
            store_act = put_slot(store_act, activated, micro_slot, is_live)
            incoming = send_back(grad_in)
            return (incoming, store_norm, store_pre, store_up, store_act, gain_acc + gain_sum)

        return backward_tick

    wide_init = jnp.zeros((MICRO, ROWS, model_width), jnp.bfloat16)
    narrow_init = jnp.zeros((MICRO, ROWS, hidden_width), jnp.bfloat16)
    carried = (
        blank_rows,
        wide_init,
        narrow_init,
        wide_init,
        narrow_init,
        jnp.zeros((model_width,), jnp.float32),
    )
    keep_count = MICRO - MICRO // 2
    is_early = section_pos < sections // 2
    tail_rows = stashed[keep_count:]
    tail_blank = jnp.zeros_like(tail_rows)
    head_rows = stashed[:keep_count]
    guest = move_mirror(jnp.where(is_early, tail_rows, tail_blank), sections)
    own_tail = jnp.where(is_early, tail_blank, tail_rows)
    split_tick = keep_count + sections // 2
    carried = lax.fori_loop(
        0, split_tick, make_tick(jnp.concatenate([head_rows, own_tail], axis=0)), carried
    )
    returned = move_mirror(jnp.where(is_early, tail_blank, guest), sections)
    restored = jnp.concatenate([head_rows, jnp.where(is_early, returned, own_tail)], axis=0)
    carried = lax.fori_loop(split_tick, tick_count, make_tick(restored), carried)
    finished, store_norm, store_pre, store_up, store_act, gain_acc = carried
    all_norm = store_norm.reshape(MICRO * ROWS, model_width)
    all_pre = store_pre.reshape(MICRO * ROWS, hidden_width)
    all_up = store_up.reshape(MICRO * ROWS, model_width)
    all_act = store_act.reshape(MICRO * ROWS, hidden_width)
    both_grads = lax.psum_scatter(
        jnp.concatenate(
            [column_product(all_norm, all_pre), column_product(all_up, all_act)], axis=1
        ).astype(jnp.bfloat16),
        "dp",
        scatter_dimension=0,
        tiled=True,
    ).astype(jnp.float32)
    in_grad = both_grads[:, :hidden_width]
    out_grad = both_grads[:, hidden_width:]
    gain_grad = lax.psum_scatter(
        gain_acc.astype(jnp.bfloat16), "dp", scatter_dimension=0, tiled=True
    ).astype(jnp.float32)
    return (in_grad[None], out_grad[None], gain_grad[None])


def solution(mesh):
    return jax.shard_map(
        local,
        mesh=mesh,
        in_specs=(
            P("dp", None),
            P("dp", None),
            P("section", None, None),
            P("section", None, None),
            P("section", None),
        ),
        out_specs=(P("section", "dp", None), P("section", "dp", None), P("section", "dp")),
        check_vma=False,
    )
```

profile of v0, /device:TPU:0, one launch (start us, length us, event | category | flops | bytes accessed | tf_op | source)
XLA Modules:
  0.0 755.8 jit_solution(4467047674511238744)
XLA Ops:
  9.0 198.3 %while.67 = (s32[]{:T(128)}, bf16[40,8192]{1,0:T(8,128)(2,1)S(1)}, bf16[4,40,8192]{2,1,0:T(8,128)(2,1)}, s32[]{:T(128)}, pred[]{:T(512)}, /*index=5*/pred[]{:T(5...) while((s32[]{:T(128)}, bf16[40,8192]{1,0:T(8,128)(2,1)S(1)}, ...), condition=%wide.region_4.5_spmd, body=%wide.region_0.4_spmd.sunk | while | flops 675123264 | bytes 25986464 | solution.py:115
  23.9 14.9 %collective-permute-done = bf16[40,8192]{1,0:T(8,128)(2,1)S(1)} collective-permute-done((bf16[40,8192]{1,0:T(8,128)(2,1)S(1)}, bf16[40,8192]{1,0:T(8,128)(2,1)S(1)}, u32[]{:S(2)}, u32[]{:S(2)}) %collective-permute-start) | collective-permute-done | bytes 655392 | tf_op jit(solution)/shard_map/while/body/eval_jaxpr/ppermute | solution.py:16
  56.7 14.0 %collective-permute-done = bf16[40,8192]{1,0:T(8,128)(2,1)S(1)} collective-permute-done((bf16[40,8192]{1,0:T(8,128)(2,1)S(1)}, bf16[40,8192]{1,0:T(8,128)(2,1)S(1)}, u32[]{:S(2)}, u32[]{:S(2)}) %collective-permute-start) | collective-permute-done | bytes 655392 | tf_op jit(solution)/shard_map/while/body/eval_jaxpr/ppermute | solution.py:16
  88.7 13.2 %collective-permute-done = bf16[40,8192]{1,0:T(8,128)(2,1)S(1)} collective-permute-done((bf16[40,8192]{1,0:T(8,128)(2,1)S(1)}, bf16[40,8192]{1,0:T(8,128)(2,1)S(1)}, u32[]{:S(2)}, u32[]{:S(2)}) %collective-permute-start) | collective-permute-done | bytes 655392 | tf_op jit(solution)/shard_map/while/body/eval_jaxpr/ppermute | solution.py:16
  119.7 12.3 %collective-permute-done = bf16[40,8192]{1,0:T(8,128)(2,1)S(1)} collective-permute-done((bf16[40,8192]{1,0:T(8,128)(2,1)S(1)}, bf16[40,8192]{1,0:T(8,128)(2,1)S(1)}, u32[]{:S(2)}, u32[]{:S(2)}) %collective-permute-start) | collective-permute-done | bytes 655392 | tf_op jit(solution)/shard_map/while/body/eval_jaxpr/ppermute | solution.py:16
  135.4 14.5 %collective-permute-start = (bf16[40,8192]{1,0:T(8,128)(2,1)S(1)}, bf16[40,8192]{1,0:T(8,128)(2,1)S(1)}, u32[]{:S(2)}, u32[]{:S(2)}) collective-permute-start(bf16[40,8192]{1,0:T(8,128)(2,1)S(1)} %get-tuple-element.1505), channel_id=1, source_target_pairs={{0,1},{1,2},{2,3},{4,5},{5,6},{6,7},{8,9},{9,10},{10,11},{12,13},{... | collective-permute-start | bytes 1966088 | tf_op jit(solution)/shard_map/while/body/eval_jaxpr/ppermute | solution.py:16
  150.0 11.4 %collective-permute-done = bf16[40,8192]{1,0:T(8,128)(2,1)S(1)} collective-permute-done((bf16[40,8192]{1,0:T(8,128)(2,1)S(1)}, bf16[40,8192]{1,0:T(8,128)(2,1)S(1)}, u32[]{:S(2)}, u32[]{:S(2)}) %collective-permute-start) | collective-permute-done | bytes 655392 | tf_op jit(solution)/shard_map/while/body/eval_jaxpr/ppermute | solution.py:16
  183.2 13.5 %collective-permute-start = (bf16[40,8192]{1,0:T(8,128)(2,1)S(1)}, bf16[40,8192]{1,0:T(8,128)(2,1)S(1)}, u32[]{:S(2)}, u32[]{:S(2)}) collective-permute-start(bf16[40,8192]{1,0:T(8,128)(2,1)S(1)} %get-tuple-element.1505), channel_id=1, source_target_pairs={{0,1},{1,2},{2,3},{4,5},{5,6},{6,7},{8,9},{9,10},{10,11},{12,13},{... | collective-permute-start | bytes 1966088 | tf_op jit(solution)/shard_map/while/body/eval_jaxpr/ppermute | solution.py:16
  211.5 25.5 %collective-permute-done.3 = bf16[2,40,8192]{2,1,0:T(8,128)(2,1)S(1)} collective-permute-done((bf16[2,40,8192]{2,1,0:T(8,128)(2,1)S(1)}, bf16[2,40,8192]{2,1,0:T(8,128)(2,1)S(1)}, u32[]{:S(2)}, u32[]{:S(2)}) %collective-permute-start.3) | collective-permute-done | bytes 1310752 | tf_op jit(solution)/shard_map/ppermute | solution.py:22
  241.8 47.9 %collective-permute-done.4 = bf16[2,40,8192]{2,1,0:T(8,128)(2,1)S(1)} collective-permute-done((bf16[2,40,8192]{2,1,0:T(8,128)(2,1)S(1)}, bf16[2,40,8192]{2,1,0:T(8,128)(2,1)S(1)}, u32[]{:S(2)}, u32[]{:S(2)}) %collective-permute-start.4) | collective-permute-done | bytes 1310752 | tf_op jit(solution)/shard_map/ppermute | solution.py:22
  290.6 27.3 %collective-permute-done.5 = bf16[2,40,8192]{2,1,0:T(8,128)(2,1)} collective-permute-done((bf16[2,40,8192]{2,1,0:T(8,128)(2,1)S(1)}, bf16[2,40,8192]{2,1,0:T(8,128)(2,1)}, u32[]{:S(2)}, u32[]{:S(2)}) %collective-permute-start.5) | collective-permute-done | bytes 1310752 | tf_op jit(solution)/shard_map/ppermute | solution.py:22
  321.1 54.8 %collective-permute-done.6 = bf16[2,40,8192]{2,1,0:T(8,128)(2,1)} collective-permute-done((bf16[2,40,8192]{2,1,0:T(8,128)(2,1)}, bf16[2,40,8192]{2,1,0:T(8,128)(2,1)}, u32[]{:S(2)}, u32[]{:S(2)}) %collective-permute-start.6) | collective-permute-done | bytes 1310752 | tf_op jit(solution)/shard_map/ppermute | solution.py:22
  385.1 134.8 %while.69 = (s32[]{:T(128)}, bf16[40,8192]{1,0:T(8,128)(2,1)}, bf16[4,40,8192]{2,1,0:T(8,128)(2,1)}, bf16[4,40,512]{2,1,0:T(8,128)(2,1)}, bf16[4,40,8192]{2,1,0:...) while((s32[]{:T(128)}, bf16[40,8192]{1,0:T(8,128)(2,1)}, ...), condition=%wide.region_11.12_spmd.clone, body=%wide.region_5.11_spmd.clone.sunk | while | flops 1015488704 | bytes 111489520 | solution.py:180
  395.4 12.3 %collective-permute-done.2 = bf16[40,8192]{1,0:T(8,128)(2,1)} collective-permute-done((bf16[40,8192]{1,0:T(8,128)(2,1)}, bf16[40,8192]{1,0:T(8,128)(2,1)}, u32[]{:S(2)}, u32[]{:S(2)}) %collective-permute-start.2) | collective-permute-done | bytes 655392 | tf_op jit(solution)/shard_map/while/body/eval_jaxpr/ppermute | solution.py:16
  418.0 12.2 %collective-permute-done.2 = bf16[40,8192]{1,0:T(8,128)(2,1)} collective-permute-done((bf16[40,8192]{1,0:T(8,128)(2,1)}, bf16[40,8192]{1,0:T(8,128)(2,1)}, u32[]{:S(2)}, u32[]{:S(2)}) %collective-permute-start.2) | collective-permute-done | bytes 655392 | tf_op jit(solution)/shard_map/while/body/eval_jaxpr/ppermute | solution.py:16
  440.5 45.9 %collective-permute-done.2 = bf16[40,8192]{1,0:T(8,128)(2,1)} collective-permute-done((bf16[40,8192]{1,0:T(8,128)(2,1)}, bf16[40,8192]{1,0:T(8,128)(2,1)}, u32[]{:S(2)}, u32[]{:S(2)}) %collective-permute-start.2) | collective-permute-done | bytes 655392 | tf_op jit(solution)/shard_map/while/body/eval_jaxpr/ppermute | solution.py:16
  490.0 12.7 %conditional.9 = (bf16[40,8192]{1,0:T(8,128)(2,1)}, bf16[40,8192]{1,0:T(8,128)(2,1)S(1)}, bf16[40,512]{1,0:T(8,128)(2,1)S(1)}, bf16[40,512]{1,0:T(8,128)(2,1)S(1)}, f32[8192]{0:T(1024)S(1)}) conditional(s32[]{:T(128)} %convert_element_type.144, () %tuple.167, (bf16[40,8192]{1,0:T(8,128)(2,1)S(1)}, bf16[4,40,8192]{2,1,0:T(8,128)(2,1)S(1)}, s32[]{:T(128)}, ...), branch_computations={%region_6.6_spmd, %region_7.10_spmd} | conditional | flops 1014448320 | bytes 90007696 | solution.py:150
  508.4 11.4 %collective-permute-done.2 = bf16[40,8192]{1,0:T(8,128)(2,1)} collective-permute-done((bf16[40,8192]{1,0:T(8,128)(2,1)}, bf16[40,8192]{1,0:T(8,128)(2,1)}, u32[]{:S(2)}, u32[]{:S(2)}) %collective-permute-start.2) | collective-permute-done | bytes 655392 | tf_op jit(solution)/shard_map/while/body/eval_jaxpr/ppermute | solution.py:16
  519.9 94.9 %while.68 = (s32[]{:T(128)}, bf16[40,8192]{1,0:T(8,128)(2,1)}, bf16[4,40,8192]{2,1,0:T(8,128)(2,1)}, bf16[4,40,512]{2,1,0:T(8,128)(2,1)}, bf16[4,40,8192]{2,1,0:...) while((s32[]{:T(128)}, bf16[40,8192]{1,0:T(8,128)(2,1)}, ...), condition=%wide.region_18.19_spmd, body=%wide.region_12.18_spmd.sunk | while | flops 1015480512 | bytes 101003736 | solution.py:185
  523.4 12.7 %conditional.8 = (bf16[40,8192]{1,0:T(8,128)(2,1)}, bf16[40,8192]{1,0:T(8,128)(2,1)S(1)}, bf16[40,512]{1,0:T(8,128)(2,1)S(1)}, bf16[40,512]{1,0:T(8,128)(2,1)S(1)}, f32[8192]{0:T(1024)S(1)}) conditional(s32[]{:T(128)} %convert_element_type.143, () %tuple.162, (bf16[40,8192]{1,0:T(8,128)(2,1)S(1)}, bf16[4,40,8192]{2,1,0:T(8,128)(2,1)S(1)}, ...), branch_computations={%region_13.13_spmd, %region_14.17_spmd} | conditional | flops 1014448320 | bytes 90007696 | solution.py:150
  555.9 12.7 %conditional.8 = (bf16[40,8192]{1,0:T(8,128)(2,1)}, bf16[40,8192]{1,0:T(8,128)(2,1)S(1)}, bf16[40,512]{1,0:T(8,128)(2,1)S(1)}, bf16[40,512]{1,0:T(8,128)(2,1)S(1)}, f32[8192]{0:T(1024)S(1)}) conditional(s32[]{:T(128)} %convert_element_type.143, () %tuple.162, (bf16[40,8192]{1,0:T(8,128)(2,1)S(1)}, bf16[4,40,8192]{2,1,0:T(8,128)(2,1)S(1)}, ...), branch_computations={%region_13.13_spmd, %region_14.17_spmd} | conditional | flops 1014448320 | bytes 90007696 | solution.py:150
  587.6 12.7 %conditional.8 = (bf16[40,8192]{1,0:T(8,128)(2,1)}, bf16[40,8192]{1,0:T(8,128)(2,1)S(1)}, bf16[40,512]{1,0:T(8,128)(2,1)S(1)}, bf16[40,512]{1,0:T(8,128)(2,1)S(1)}, f32[8192]{0:T(1024)S(1)}) conditional(s32[]{:T(128)} %convert_element_type.143, () %tuple.162, (bf16[40,8192]{1,0:T(8,128)(2,1)S(1)}, bf16[4,40,8192]{2,1,0:T(8,128)(2,1)S(1)}, ...), branch_computations={%region_13.13_spmd, %region_14.17_spmd} | conditional | flops 1014448320 | bytes 90007696 | solution.py:150
  630.5 22.3 %all-reduce = bf16[8192]{0:T(1024)(128)(2,1)S(1)} all-reduce(bf16[8192]{0:T(1024)(128)(2,1)S(1)} %convert_element_type.101), channel_id=3, replica_groups=mesh['dp'=8,'section'=4] {'dp'}, use_global_device_ids=true, to_apply=%region_20.21.clone | all-reduce | flops 8192 | bytes 32768
  653.4 87.2 %reduce-scatter.2.cloned.1.call-done = bf16[1024,1024]{0,1:T(8,128)(2,1)} async-done(((bf16[8192,1024]{0,1:T(8,128)(2,1)}), bf16[1024,1024]{0,1:T(8,128)(2,1)}) %reduce-scatter.2.cloned.1.call-update) | async-done | bytes 2097168 | tf_op jit(solution)/shard_map/reduce_scatter | solution.py:191
  (277 shorter events, 343.3 us)
Async XLA Ops:
  7.2 733.4 %reduce-scatter.2.cloned.1.call-start = ((), (), s32[]{:S(2)}) async-start(), calls=%async_computation.1 | async-start | bytes 18874368 | tf_op jit(solution)/shard_map/reduce_scatter | solution.py:191
  22.5 16.2 %collective-permute-start = (bf16[40,8192]{1,0:T(8,128)(2,1)S(1)}, bf16[40,8192]{1,0:T(8,128)(2,1)S(1)}, u32[]{:S(2)}, u32[]{:S(2)}) collective-permute-start(bf16[40,8192]{1,0:T(8,128)(2,1)S(1)} %get-tuple-element.1505), channel_id=1, source_target_pairs={{0,1},{1,2},{2,3},{4,5},{5,6},{6,7},{8,9},{9,10},{10,11},{12,13},{... | collective-permute-start | bytes 1966088 | tf_op jit(solution)/shard_map/while/body/eval_jaxpr/ppermute | solution.py:16
  52.3 18.4 %collective-permute-start = (bf16[40,8192]{1,0:T(8,128)(2,1)S(1)}, bf16[40,8192]{1,0:T(8,128)(2,1)S(1)}, u32[]{:S(2)}, u32[]{:S(2)}) collective-permute-start(bf16[40,8192]{1,0:T(8,128)(2,1)S(1)} %get-tuple-element.1505), channel_id=1, source_target_pairs={{0,1},{1,2},{2,3},{4,5},{5,6},{6,7},{8,9},{9,10},{10,11},{12,13},{... | collective-permute-start | bytes 1966088 | tf_op jit(solution)/shard_map/while/body/eval_jaxpr/ppermute | solution.py:16
  84.2 17.6 %collective-permute-start = (bf16[40,8192]{1,0:T(8,128)(2,1)S(1)}, bf16[40,8192]{1,0:T(8,128)(2,1)S(1)}, u32[]{:S(2)}, u32[]{:S(2)}) collective-permute-start(bf16[40,8192]{1,0:T(8,128)(2,1)S(1)} %get-tuple-element.1505), channel_id=1, source_target_pairs={{0,1},{1,2},{2,3},{4,5},{5,6},{6,7},{8,9},{9,10},{10,11},{12,13},{... | collective-permute-start | bytes 1966088 | tf_op jit(solution)/shard_map/while/body/eval_jaxpr/ppermute | solution.py:16
  115.3 16.7 %collective-permute-start = (bf16[40,8192]{1,0:T(8,128)(2,1)S(1)}, bf16[40,8192]{1,0:T(8,128)(2,1)S(1)}, u32[]{:S(2)}, u32[]{:S(2)}) collective-permute-start(bf16[40,8192]{1,0:T(8,128)(2,1)S(1)} %get-tuple-element.1505), channel_id=1, source_target_pairs={{0,1},{1,2},{2,3},{4,5},{5,6},{6,7},{8,9},{9,10},{10,11},{12,13},{... | collective-permute-start | bytes 1966088 | tf_op jit(solution)/shard_map/while/body/eval_jaxpr/ppermute | solution.py:16
  135.4 26.0 %collective-permute-start = (bf16[40,8192]{1,0:T(8,128)(2,1)S(1)}, bf16[40,8192]{1,0:T(8,128)(2,1)S(1)}, u32[]{:S(2)}, u32[]{:S(2)}) collective-permute-start(bf16[40,8192]{1,0:T(8,128)(2,1)S(1)} %get-tuple-element.1505), channel_id=1, source_target_pairs={{0,1},{1,2},{2,3},{4,5},{5,6},{6,7},{8,9},{9,10},{10,11},{12,13},{... | collective-permute-start | bytes 1966088 | tf_op jit(solution)/shard_map/while/body/eval_jaxpr/ppermute | solution.py:16
  164.8 15.0 %collective-permute-start = (bf16[40,8192]{1,0:T(8,128)(2,1)S(1)}, bf16[40,8192]{1,0:T(8,128)(2,1)S(1)}, u32[]{:S(2)}, u32[]{:S(2)}) collective-permute-start(bf16[40,8192]{1,0:T(8,128)(2,1)S(1)} %get-tuple-element.1505), channel_id=1, source_target_pairs={{0,1},{1,2},{2,3},{4,5},{5,6},{6,7},{8,9},{9,10},{10,11},{12,13},{... | collective-permute-start | bytes 1966088 | tf_op jit(solution)/shard_map/while/body/eval_jaxpr/ppermute | solution.py:16
  183.2 24.2 %collective-permute-start = (bf16[40,8192]{1,0:T(8,128)(2,1)S(1)}, bf16[40,8192]{1,0:T(8,128)(2,1)S(1)}, u32[]{:S(2)}, u32[]{:S(2)}) collective-permute-start(bf16[40,8192]{1,0:T(8,128)(2,1)S(1)} %get-tuple-element.1505), channel_id=1, source_target_pairs={{0,1},{1,2},{2,3},{4,5},{5,6},{6,7},{8,9},{9,10},{10,11},{12,13},{... | collective-permute-start | bytes 1966088 | tf_op jit(solution)/shard_map/while/body/eval_jaxpr/ppermute | solution.py:16
  207.4 168.5 %copy-start.7 = (bf16[4,40,8192]{2,1,0:T(8,128)(2,1)S(1)}, bf16[4,40,8192]{2,1,0:T(8,128)(2,1)}, u32[]{:S(2)}) copy-start(bf16[4,40,8192]{2,1,0:T(8,128)(2,1)} %get-tuple-element.889) | copy-start | bytes 7864324
  208.9 28.0 %collective-permute-start.3 = (bf16[2,40,8192]{2,1,0:T(8,128)(2,1)S(1)}, bf16[2,40,8192]{2,1,0:T(8,128)(2,1)S(1)}, u32[]{:S(2)}, u32[]{:S(2)}) collective-permute-start(bf16[2,40,8192]{2,1,0:T(8,128)(2,1)S(1)} %broadcast_select_fusion.2), channel_id=1, source_target_pairs={{0,1},{1,0},{2,3},{3,2},{4,5},{5,4},{6,7},{7,6},{8,9},{9,8},{10,11... | collective-permute-start | bytes 3932168 | tf_op jit(solution)/shard_map/ppermute | solution.py:22
  237.0 52.7 %collective-permute-start.4 = (bf16[2,40,8192]{2,1,0:T(8,128)(2,1)S(1)}, bf16[2,40,8192]{2,1,0:T(8,128)(2,1)S(1)}, u32[]{:S(2)}, u32[]{:S(2)}) collective-permute-start(bf16[2,40,8192]{2,1,0:T(8,128)(2,1)S(1)} %collective-permute-done.3), channel_id=1, source_target_pairs={{0,2},{1,3},{2,0},{3,1},{4,6},{5,7},{6,4},{7,5},{8,10},{9,11},{10,... | collective-permute-start | bytes 3932168 | tf_op jit(solution)/shard_map/ppermute | solution.py:22
  289.8 28.1 %collective-permute-start.5 = (bf16[2,40,8192]{2,1,0:T(8,128)(2,1)S(1)}, bf16[2,40,8192]{2,1,0:T(8,128)(2,1)}, u32[]{:S(2)}, u32[]{:S(2)}) collective-permute-start(bf16[2,40,8192]{2,1,0:T(8,128)(2,1)S(1)} %broadcast_select_fusion.1), channel_id=1, source_target_pairs={{0,1},{1,0},{2,3},{3,2},{4,5},{5,4},{6,7},{7,6},{8,9},{9,8},{10,11... | collective-permute-start | bytes 3932168 | tf_op jit(solution)/shard_map/ppermute | solution.py:22
  317.9 58.0 %collective-permute-start.6 = (bf16[2,40,8192]{2,1,0:T(8,128)(2,1)}, bf16[2,40,8192]{2,1,0:T(8,128)(2,1)}, u32[]{:S(2)}, u32[]{:S(2)}) collective-permute-start(bf16[2,40,8192]{2,1,0:T(8,128)(2,1)} %collective-permute-done.5), channel_id=1, source_target_pairs={{0,2},{1,3},{2,0},{3,1},{4,6},{5,7},{6,4},{7,5},{8,10},{9,11},{10,... | collective-permute-start | bytes 3932168 | tf_op jit(solution)/shard_map/ppermute | solution.py:22
  389.7 18.0 %collective-permute-start.2 = (bf16[40,8192]{1,0:T(8,128)(2,1)}, bf16[40,8192]{1,0:T(8,128)(2,1)}, u32[]{:S(2)}, u32[]{:S(2)}) collective-permute-start(bf16[40,8192]{1,0:T(8,128)(2,1)} %get-tuple-element.1327), channel_id=1, source_target_pairs={{1,0},{2,1},{3,2},{5,4},{6,5},{7,6},{9,8},{10,9},{11,10},{13,12},{... | collective-permute-start | bytes 1966088 | tf_op jit(solution)/shard_map/while/body/eval_jaxpr/ppermute | solution.py:16
  412.3 17.9 %collective-permute-start.2 = (bf16[40,8192]{1,0:T(8,128)(2,1)}, bf16[40,8192]{1,0:T(8,128)(2,1)}, u32[]{:S(2)}, u32[]{:S(2)}) collective-permute-start(bf16[40,8192]{1,0:T(8,128)(2,1)} %get-tuple-element.1327), channel_id=1, source_target_pairs={{1,0},{2,1},{3,2},{5,4},{6,5},{7,6},{9,8},{10,9},{11,10},{13,12},{... | collective-permute-start | bytes 1966088 | tf_op jit(solution)/shard_map/while/body/eval_jaxpr/ppermute | solution.py:16
  434.8 51.6 %collective-permute-start.2 = (bf16[40,8192]{1,0:T(8,128)(2,1)}, bf16[40,8192]{1,0:T(8,128)(2,1)}, u32[]{:S(2)}, u32[]{:S(2)}) collective-permute-start(bf16[40,8192]{1,0:T(8,128)(2,1)} %get-tuple-element.1327), channel_id=1, source_target_pairs={{1,0},{2,1},{3,2},{5,4},{6,5},{7,6},{9,8},{10,9},{11,10},{13,12},{... | collective-permute-start | bytes 1966088 | tf_op jit(solution)/shard_map/while/body/eval_jaxpr/ppermute | solution.py:16
  490.6 7.2 slice-start
  502.8 17.1 %collective-permute-start.2 = (bf16[40,8192]{1,0:T(8,128)(2,1)}, bf16[40,8192]{1,0:T(8,128)(2,1)}, u32[]{:S(2)}, u32[]{:S(2)}) collective-permute-start(bf16[40,8192]{1,0:T(8,128)(2,1)} %get-tuple-element.1327), channel_id=1, source_target_pairs={{1,0},{2,1},{3,2},{5,4},{6,5},{7,6},{9,8},{10,9},{11,10},{13,12},{... | collective-permute-start | bytes 1966088 | tf_op jit(solution)/shard_map/while/body/eval_jaxpr/ppermute | solution.py:16
  523.9 7.2 slice-start.2
  536.1 16.2 %collective-permute-start.1 = (bf16[40,8192]{1,0:T(8,128)(2,1)}, bf16[40,8192]{1,0:T(8,128)(2,1)}, u32[]{:S(2)}, u32[]{:S(2)}) collective-permute-start(bf16[40,8192]{1,0:T(8,128)(2,1)} %get-tuple-element.1304), channel_id=1, source_target_pairs={{1,0},{2,1},{3,2},{5,4},{6,5},{7,6},{9,8},{10,9},{11,10},{13,12},{... | collective-permute-start | bytes 1966088 | tf_op jit(solution)/shard_map/while/body/eval_jaxpr/ppermute | solution.py:16
  556.4 7.2 slice-start.2
  568.6 15.4 %collective-permute-start.1 = (bf16[40,8192]{1,0:T(8,128)(2,1)}, bf16[40,8192]{1,0:T(8,128)(2,1)}, u32[]{:S(2)}, u32[]{:S(2)}) collective-permute-start(bf16[40,8192]{1,0:T(8,128)(2,1)} %get-tuple-element.1304), channel_id=1, source_target_pairs={{1,0},{2,1},{3,2},{5,4},{6,5},{7,6},{9,8},{10,9},{11,10},{13,12},{... | collective-permute-start | bytes 1966088 | tf_op jit(solution)/shard_map/while/body/eval_jaxpr/ppermute | solution.py:16
  588.1 7.2 slice-start.2
  600.3 14.5 %collective-permute-start.1 = (bf16[40,8192]{1,0:T(8,128)(2,1)}, bf16[40,8192]{1,0:T(8,128)(2,1)}, u32[]{:S(2)}, u32[]{:S(2)}) collective-permute-start(bf16[40,8192]{1,0:T(8,128)(2,1)} %get-tuple-element.1304), channel_id=1, source_target_pairs={{1,0},{2,1},{3,2},{5,4},{6,5},{7,6},{9,8},{10,9},{11,10},{13,12},{... | collective-permute-start | bytes 1966088 | tf_op jit(solution)/shard_map/while/body/eval_jaxpr/ppermute | solution.py:16
  (36 other events, 126.6 us)
Sparse Core Ops, SparseCore 0:
  628.7 111.8 reduce-scatter.1
where the time goes:
time: 759 us; the launch traced here: 756 us
  waiting for transfers between devices  441 us (58%)
  matrix products  85.2 us (11%)
  starting transfers between devices  67.4 us (9%)
  other arithmetic  66.7 us (9%)
  local copies, waits for them, and re-layouts  57.9 us (8%)
  blocking collectives  22.3 us (3%)
  between operations  14.8 us (2%)
    ppermute x14, waiting for transfers between devices, from_behind(): return lax.ppermute(block, axis, route)  198 us
    ppermute x4, waiting for transfers between devices, from_partner(): return lax.ppermute(value, axis, pairs)  156 us
    reduce_scatter x1, waiting for transfers between devices, local(): lax.psum_scatter(jnp.concatenate([column_product(all_norm, all_pre), colu...  87.2 us
    ppermute x14, starting transfers between devices, from_behind(): return lax.ppermute(block, axis, route)  56 us
    dynamic_update_slice x28, other arithmetic, put_slot(): lax.dynamic_update_index_in_dim(stored, jnp.where(is_live, fresh, kept_ro...  43.9 us
    dot_general x4, matrix products, layer_forward(): lax.dot_general(activated, w_out, (((1,), (1,)), ((), ())), preferred_ele...  39.5 us
    dynamic_slice x35, local copies, waits for them, and re-layouts, put_slot(): kept_rows = lax.dynamic_index_in_dim(stored, micro_slot, 0, keepdims=False)  35.3 us
    unnamed x1, blocking collectives  22.3 us
  transfers between devices with their start and end apart: 19, of which 19 were waited for; matrix products, arithmetic and copies ran while one was open for 4% of the time, Pallas kernels for 0%

commit v1 on v0

v1 whole, which is shorter than its diff:
```python
import functools

import jax
import jax.numpy as jnp
from jax import lax
from jax.experimental import pallas as pl
from jax.experimental.pallas import tpu as pltpu
from jax.sharding import PartitionSpec as P

ROWS = 16
CHUNK = 2048
DELAY = 2
EPSILON = 1e-05
MESH = pl.DeviceIdType.MESH


def nt_dot(left, right):
    return lax.dot_general(
        left, right, (((1,), (1,)), ((), ())), preferred_element_type=jnp.float32
    )


def column_product(left, right):
    return lax.dot_general(
        left, right, (((0,), (0,)), ((), ())), preferred_element_type=jnp.float32
    )


def relay_kernel(
    sections,
    micros,
    x_ref,
    c_ref,
    win_hbm,
    wout_hbm,
    gain_ref,
    n_out,
    g_out,
    act_out,
    du_out,
    gg_out,
    win,
    wout,
    stash,
    up,
    out_f,
    out_b,
    normed,
    pre,
    scale,
    w_sem,
    f_recv,
    b_recv,
    f_send,
    b_send,
    o_sem,
):
    width = stash.shape[2]
    chunks = width // CHUNK
    pos = lax.axis_index("section")
    is_first = pos == 0
    is_last = pos == sections - 1
    not_first = pos > 0
    not_last = pos < sections - 1

    win_copy = pltpu.make_async_copy(win_hbm, win, w_sem.at[0])
    wout_copy = pltpu.make_async_copy(wout_hbm, wout, w_sem.at[1])
    win_copy.start()

    @pl.when(is_first)
    def _():
        @pl.loop(0, micros)
        def _(m):
            pltpu.make_async_copy(x_ref.at[m], stash.at[m], f_recv.at[m]).start()

    wout_copy.start()

    @pl.when(is_last)
    def _():
        @pl.loop(0, micros)
        def _(m):
            pltpu.make_async_copy(c_ref.at[m], up.at[m], b_recv.at[m]).start()

    barrier = pltpu.get_barrier_semaphore()

    @pl.when(not_first)
    def _():
        pl.semaphore_signal(
            barrier, inc=1, device_id={"section": pos - 1}, device_id_type=MESH
        )

    @pl.when(not_last)
    def _():
        pl.semaphore_signal(
            barrier, inc=1, device_id={"section": pos + 1}, device_id_type=MESH
        )

    pl.semaphore_wait(barrier, not_first.astype(jnp.int32) + not_last.astype(jnp.int32))

    gg_out[...] = jnp.zeros_like(gg_out)
    win_copy.wait()
    wout_copy.wait()

    def cols(k):
        return pl.ds(pl.multiple_of(k * CHUNK, CHUNK), CHUNK)

    def send_forward(m):
        return pltpu.make_async_remote_copy(
            src_ref=out_f.at[m],
            dst_ref=stash.at[m],
            send_sem=f_send.at[m],
            recv_sem=f_recv.at[m],
            device_id={"section": pos + 1},
            device_id_type=MESH,
        )

    def send_backward(m):
        return pltpu.make_async_remote_copy(
            src_ref=out_b.at[m],
            dst_ref=up.at[m],
            send_sem=b_send.at[m],
            recv_sem=b_recv.at[m],
            device_id={"section": pos - 1},
            device_id_type=MESH,
        )

    def forward(m):
        pltpu.make_async_copy(stash.at[m], stash.at[m], f_recv.at[m]).wait()

        def add_squares(k, total):
            h = stash[m, :, cols(k)].astype(jnp.float32)
            return total + jnp.sum(h * h, axis=1, keepdims=True)

        total = lax.fori_loop(
            0, chunks, add_squares, jnp.zeros((ROWS, 1), jnp.float32)
        )
        inv = lax.rsqrt(total / width + EPSILON)

        def project(k, acc):
            h = stash[m, :, cols(k)].astype(jnp.float32)
            n = (h * inv * gain_ref[:, cols(k)]).astype(jnp.bfloat16)
            normed[m, :, cols(k)] = n
            return acc + jnp.dot(
                n, win[cols(k), :], preferred_element_type=jnp.float32
            )

        u = lax.fori_loop(
            0, chunks, project, jnp.zeros((ROWS, win.shape[1]), jnp.float32)
        )
        act = (u * jax.nn.sigmoid(u)).astype(jnp.bfloat16)
        pre[m] = u
        scale[m] = jnp.broadcast_to(inv, scale.shape[1:])
        act_out[m] = act

        @pl.when(not_last)
        def _():
            @pl.loop(0, chunks)
            def _(k):
                h = stash[m, :, cols(k)].astype(jnp.float32)
                out_f[m, :, cols(k)] = (h + nt_dot(act, wout[cols(k), :])).astype(
                    jnp.bfloat16
                )

            send_forward(m).start()

    def backward(m):
        pltpu.make_async_copy(up.at[m], up.at[m], b_recv.at[m]).wait()

        def project(k, acc):
            return acc + jnp.dot(
                up[m, :, cols(k)], wout[cols(k), :], preferred_element_type=jnp.float32
            )

        da = lax.fori_loop(
            0, chunks, project, jnp.zeros((ROWS, win.shape[1]), jnp.float32)
        )
        u = pre[m]
        inv = scale[m][:, :1]
        sig = jax.nn.sigmoid(u)
        du = (da * sig * (1.0 + u * (1.0 - sig))).astype(jnp.bfloat16)
        du_out[m] = du
        centered = jnp.sum(du.astype(jnp.float32) * u, axis=1, keepdims=True) / (
            inv * width
        )
        pull = inv * inv * inv * centered

        @pl.loop(0, chunks)
        def _(k):
            h = stash[m, :, cols(k)].astype(jnp.float32)
            dn = nt_dot(du, win[cols(k), :])
            rows = dn * h * inv
            gg_out[:, cols(k)] += rows[:8] + rows[8:]

            @pl.when(not_first)
            def _():
                g = up[m, :, cols(k)].astype(jnp.float32)
                out_b[m, :, cols(k)] = (
                    g + inv * (dn * gain_ref[:, cols(k)]) - h * pull
                ).astype(jnp.bfloat16)

        @pl.when(not_first)
        def _():
            send_backward(m).start()

        pltpu.make_async_copy(normed.at[m], n_out.at[m], o_sem.at[0, m]).start()
        pltpu.make_async_copy(up.at[m], g_out.at[m], o_sem.at[1, m]).start()

    @pl.loop(0, micros + 2 * DELAY * (sections - 1))
    def _(tick):
        mf = tick - DELAY * pos
        mb = tick - DELAY * (2 * (sections - 1) - pos)

        @pl.when((mf >= 0) & (mf < micros))
        def _():
            forward(mf)

        @pl.when((mb >= 0) & (mb < micros))
        def _():
            backward(mb)

    @pl.loop(0, micros)
    def _(m):
        pltpu.make_async_copy(normed.at[m], n_out.at[m], o_sem.at[0, m]).wait()
        pltpu.make_async_copy(up.at[m], g_out.at[m], o_sem.at[1, m]).wait()

        @pl.when(not_last)
        def _():
            send_forward(m).wait_send()

        @pl.when(not_first)
        def _():
            send_backward(m).wait_send()


def local(sections, inputs, cotangent, weight_in, weight_out, norm_gains):
    tokens, width = inputs.shape
    hidden = weight_in.shape[2]
    micros = tokens // ROWS
    wide = jax.ShapeDtypeStruct((micros, ROWS, width), jnp.bfloat16)
    narrow = jax.ShapeDtypeStruct((micros, ROWS, hidden), jnp.bfloat16)
    any_spec = pl.BlockSpec(memory_space=pl.ANY)
    vmem_spec = pl.BlockSpec(memory_space=pltpu.VMEM)
    wide_scratch = pltpu.VMEM((micros, ROWS, width), jnp.bfloat16)
    weight_scratch = pltpu.VMEM((width, hidden), jnp.bfloat16)
    dma = pltpu.SemaphoreType.DMA
    all_norm, all_up, all_act, all_pre, gain_acc = pl.pallas_call(
        functools.partial(relay_kernel, sections, micros),
        out_shape=(
            wide,
            wide,
            narrow,
            narrow,
            jax.ShapeDtypeStruct((8, width), jnp.float32),
        ),
        in_specs=[any_spec] * 4 + [vmem_spec],
        out_specs=(any_spec, any_spec, vmem_spec, vmem_spec, vmem_spec),
        scratch_shapes=[
            weight_scratch,
            weight_scratch,
            wide_scratch,
            wide_scratch,
            wide_scratch,
            wide_scratch,
            wide_scratch,
            pltpu.VMEM((micros, ROWS, hidden), jnp.float32),
            pltpu.VMEM((micros, ROWS, 128), jnp.float32),
            dma((2,)),
            dma((micros,)),
            dma((micros,)),
            dma((micros,)),
            dma((micros,)),
            dma((2, micros)),
        ],
        compiler_params=pltpu.CompilerParams(
            collective_id=0, has_side_effects=True, vmem_limit_bytes=60 * 2**20
        ),
    )(
        inputs.reshape(micros, ROWS, width),
        cotangent.reshape(micros, ROWS, width),
        weight_in[0],
        weight_out[0],
        norm_gains,
    )
    all_norm = all_norm.reshape(tokens, width)
    all_up = all_up.reshape(tokens, width)
    all_act = all_act.reshape(tokens, hidden)
    all_pre = all_pre.reshape(tokens, hidden)
    both_grads = lax.psum_scatter(
        jnp.concatenate(
            [column_product(all_norm, all_pre), column_product(all_up, all_act)], axis=1
        ).astype(jnp.bfloat16),
        "dp",
        scatter_dimension=0,
        tiled=True,
    ).astype(jnp.float32)
    gain_grad = lax.psum_scatter(
        jnp.sum(gain_acc, axis=0).astype(jnp.bfloat16), "dp", scatter_dimension=0, tiled=True
    ).astype(jnp.float32)
    return (both_grads[:, :hidden][None], both_grads[:, hidden:][None], gain_grad[None])


def solution(mesh):
    return jax.shard_map(
        functools.partial(local, mesh.shape["section"]),
        mesh=mesh,
        in_specs=(
            P("dp", None),
            P("dp", None),
            P("section", None, None),
            P("section", None, None),
            P("section", None),
        ),
        out_specs=(P("section", "dp", None), P("section", "dp", None), P("section", "dp")),
        check_vma=False,
    )
```

time: 759 us -> 308 us (0.41)
  waiting for transfers between devices: 441 us -> 89.2 us
  Pallas kernels: 0 us -> 157 us
  matrix products: 85.2 us -> 6.66 us
  starting transfers between devices: 67.4 us -> 0.04 us
  other arithmetic: 66.7 us -> 9.84 us
  local copies, waits for them, and re-layouts: 57.9 us -> 7.68 us
    ppermute x18 -> x0, waiting for transfers between devices: 354 us -> none  [the longest x14 198 us: from_behind(): return lax.ppermute(block, axis, route)]
    pallas_call x0 -> x1, Pallas kernels: none -> 157 us  [local(): pl.pallas_call(functools.partial(relay_kernel, sections, micros), out_sha...]
    dot_general x16 -> x0, matrix products: 78.5 us -> none  [the longest x4 39.5 us: layer_forward(): lax.dot_general(activated, w_out, (((1,), (1,)), ((), ())), preferred_ele...]
    ppermute x18 -> x0, starting transfers between devices: 67.3 us -> none  [the longest x14 56 us: from_behind(): return lax.ppermute(block, axis, route)]
    dynamic_update_slice x28 -> x0, other arithmetic: 43.9 us -> none  [put_slot(): lax.dynamic_update_index_in_dim(stored, jnp.where(is_live, fresh, kept_ro...]
    dynamic_slice x35 -> x0, local copies, waits for them, and re-layouts: 35.3 us -> none  [put_slot(): kept_rows = lax.dynamic_index_in_dim(stored, micro_slot, 0, keepdims=False)]
    another operation x23 -> x0, local copies, waits for them, and re-layouts: 9.28 us -> none
  transfers between devices with their start and end apart: 19 -> 1, of which waited for: 19 -> 1; matrix products, arithmetic and copies ran while one was open for 4% -> 0% of each run, Pallas kernels for 0% -> 0%
where the time goes in v1:
time: 308 us; the launch traced here: 307 us
  Pallas kernels  157 us (51%)
  waiting for transfers between devices  89.2 us (29%)
  blocking collectives  22.3 us (7%)
  between operations  14.8 us (5%)
  other arithmetic  9.84 us (3%)
  local copies, waits for them, and re-layouts  7.68 us (2%)
  matrix products  6.66 us (2%)
    pallas_call x1, Pallas kernels, local(): pl.pallas_call(functools.partial(relay_kernel, sections, micros), out_sha...  157 us
    reduce_scatter x1, waiting for transfers between devices, local(): lax.psum_scatter(jnp.concatenate([column_product(all_norm, all_pre), colu...  89.2 us
    unnamed x1, blocking collectives  22.3 us
    concatenate x1, other arithmetic, local(): jnp.concatenate([column_product(all_norm, all_pre), column_product(all_up...  7.14 us
    dot_general x2, matrix products, column_product(): lax.dot_general(left, right, (((0,), (0,)), ((), ())), preferred_element_...  6.66 us
  transfers between devices with their start and end apart: 1, of which 1 were waited for; matrix products, arithmetic and copies ran while one was open for 0% of the time, Pallas kernels for 0%

profile of v1, /device:TPU:0, one launch (start us, length us, event | category | flops | bytes accessed | tf_op | source)
XLA Modules:
  0.0 307.5 jit_solution(1610925415961878632)
XLA Ops:
  7.2 0.0 reduce-scatter.2.cloned.1.call-start
  7.2 157.0 %shard_map.76 = (bf16[10,16,8192]{2,1,0:T(8,128)(2,1)}, bf16[10,16,8192]{2,1,0:T(8,128)(2,1)}, bf16[10,16,512]{2,1,0:T(8,128)(2,1)}, bf16[10,16,512]{2,1,0:T(8,128)(2,1)}, f32[8,8192]{1,0:T(8,128)}) custom-call(bf16[10,16,8192]{2,1,0:T(8,128)(2,1)} %bitcast.20, bf16[10,16,8192]{2,1,0:T(8,128)(2,1)} %bitcast.21, bf16[8192,512]{1,0:T(8,128)(2,1)} %bitcast.18, ...), custom_call_target="tpu_custom_call" | custom-call | tf_op jit(solution)/shard_map/pallas_call | solution.py:246
  164.2 0.0 copy-start
  164.2 0.0 copy-start.2
  164.2 4.3 %bitcast_convert_fusion.1 = bf16[8192,512]{0,1:T(8,128)(2,1)S(1)} fusion(bf16[10,16,8192]{2,1,0:T(8,128)(2,1)} %get-tuple-element.8, bf16[10,16,512]{2,1,0:T(8,128)(2,1)} %get-tuple-element.9), kind=kOutput, calls=%fused_computation.2 | convolution fusion | flops 1346371584 | bytes 11173888 | tf_op jit(solution)/shard_map/dot_general | solution.py:24
  168.5 0.0 copy-done
  168.5 0.0 copy-done.2
  168.5 2.4 bitcast_convert_fusion
  170.9 7.1 %pad_maximum_fusion = bf16[8192,1024]{0,1:T(8,128)(2,1)} fusion(bf16[8192,512]{0,1:T(8,128)(2,1)S(1)} %bitcast_convert_fusion, bf16[8192,512]{0,1:T(8,128)(2,1)S(1)} %bitcast_convert_fusion.1), kind=kLoop, calls=%fused_computation | loop fusion | flops 33554432 | bytes 33554432 | tf_op jit(solution)/shard_map/concatenate | solution.py:289
  178.0 0.0 copy-start.3
  178.0 0.0 copy-start.1
  178.0 0.0 reduce-scatter.2.cloned.1.call-update
  178.1 0.6 copy-done.3
  178.7 0.6 dynamic-slice
  179.9 0.0 copy-done.1
  179.9 0.1 reduce_sum.9
  180.0 22.3 %all-reduce = bf16[8192]{0:T(1024)(128)(2,1)S(1)} all-reduce(bf16[8192]{0:T(1024)(128)(2,1)S(1)} %reduce_sum.9), channel_id=3, replica_groups=mesh['dp'=8,'section'=4] {'dp'}, use_global_device_ids=true, to_apply=%region_2.0.clone | all-reduce | flops 8192 | bytes 32768
  202.3 0.6 dynamic-slice_convert_fusion
  202.9 89.2 %reduce-scatter.2.cloned.1.call-done = bf16[1024,1024]{0,1:T(8,128)(2,1)} async-done(((bf16[8192,1024]{0,1:T(8,128)(2,1)}), bf16[1024,1024]{0,1:T(8,128)(2,1)}) %reduce-scatter.2.cloned.1.call-update) | async-done | bytes 2097168 | tf_op jit(solution)/shard_map/reduce_scatter | solution.py:288
  292.1 2.0 convert_element_type.8
  294.1 1.8 slice_bitcast_fusion
  295.9 2.9 copy.11
  298.8 1.8 copy.10
Async XLA Ops:
  7.2 284.9 %reduce-scatter.2.cloned.1.call-start = ((), (), s32[]{:S(2)}) async-start(), calls=%async_computation.1 | async-start | bytes 18874368 | tf_op jit(solution)/shard_map/reduce_scatter | solution.py:288
  164.2 4.3 %copy-start = (bf16[10,16,8192]{2,1,0:T(8,128)(2,1)S(1)}, bf16[10,16,8192]{2,1,0:T(8,128)(2,1)}, u32[]{:S(2)}) copy-start(bf16[10,16,8192]{2,1,0:T(8,128)(2,1)} %get-tuple-element.10) | copy-start | bytes 7864324
  164.2 4.3 %copy-start.2 = (bf16[10,16,512]{2,1,0:T(8,128)(2,1)S(1)}, bf16[10,16,512]{2,1,0:T(8,128)(2,1)}, u32[]{:S(2)}) copy-start(bf16[10,16,512]{2,1,0:T(8,128)(2,1)} %get-tuple-element.11) | copy-start | bytes 491524
  178.0 0.7 copy-start.3
  178.0 1.9 copy-start.1
Sparse Core Ops, SparseCore 0:
  178.2 113.8 reduce-scatter.1

commit v2 on v1

--- a/solution.py
+++ b/solution.py
@@ -28,24 +28,27 @@
 
 def relay_kernel(
     sections,
+    replicas,
     micros,
     x_ref,
     c_ref,
     win_hbm,
     wout_hbm,
     gain_ref,
-    n_out,
-    g_out,
-    act_out,
-    du_out,
-    gg_out,
+    all_h,
+    all_g,
+    all_act,
+    all_du,
+    all_gain,
     win,
     wout,
     stash,
     up,
     out_f,
     out_b,
-    normed,
+    act_buf,
+    du_buf,
+    gain_acc,
     pre,
     scale,
     w_sem,
@@ -53,11 +56,14 @@
     b_recv,
     f_send,
     b_send,
-    o_sem,
+    x_recv,
+    x_send,
 ):
     width = stash.shape[2]
     chunks = width // CHUNK
     pos = lax.axis_index("section")
+    block = width // replicas
+    me = lax.axis_index("dp")
     is_first = pos == 0
     is_last = pos == sections - 1
     not_first = pos > 0
@@ -95,11 +101,21 @@
             barrier, inc=1, device_id={"section": pos + 1}, device_id_type=MESH
         )
 
-    pl.semaphore_wait(barrier, not_first.astype(jnp.int32) + not_last.astype(jnp.int32))
-
-    gg_out[...] = jnp.zeros_like(gg_out)
-    win_copy.wait()
-    wout_copy.wait()
+    @pl.loop(1, replicas)
+    def _(step):
+        pl.semaphore_signal(
+            barrier,
+            inc=1,
+            device_id={"dp": lax.rem(me + step, replicas)},
+            device_id_type=MESH,
+        )
+
+    pl.semaphore_wait(
+        barrier,
+        replicas - 1 + not_first.astype(jnp.int32) + not_last.astype(jnp.int32),
+    )
+
+    gain_acc[...] = jnp.zeros_like(gain_acc)
 
     def cols(k):
         return pl.ds(pl.multiple_of(k * CHUNK, CHUNK), CHUNK)
@@ -124,33 +140,60 @@
             device_id_type=MESH,
         )
 
+    def share(kind, src_of, dst):
+        pltpu.make_async_copy(src_of(me), dst, x_recv.at[kind]).start()
+
+        @pl.loop(1, replicas)
+        def _(step):
+            peer = lax.rem(me + step, replicas)
+            pltpu.make_async_remote_copy(
+                src_ref=src_of(peer),
+                dst_ref=dst,
+                send_sem=x_send.at[kind],
+                recv_sem=x_recv.at[kind],
+                device_id={"dp": peer},
+                device_id_type=MESH,
+            ).start()
+
+    def part(owner):
+        return pl.ds(pl.multiple_of(owner * block, block), block)
+
     def forward(m):
         pltpu.make_async_copy(stash.at[m], stash.at[m], f_recv.at[m]).wait()
 
-        def add_squares(k, total):
+        @pl.when(m == 0)
+        def _():
+            win_copy.wait()
+
+        def project(k, carry):
+            total, acc = carry
             h = stash[m, :, cols(k)].astype(jnp.float32)
-            return total + jnp.sum(h * h, axis=1, keepdims=True)
-
-        total = lax.fori_loop(
-            0, chunks, add_squares, jnp.zeros((ROWS, 1), jnp.float32)
+            scaled = (h * gain_ref[:, cols(k)]).astype(jnp.bfloat16)
+            return (
+                total + jnp.sum(h * h, axis=1, keepdims=True),
+                acc
+                + jnp.dot(scaled, win[cols(k), :], preferred_element_type=jnp.float32),
+            )
+
+        total, u = lax.fori_loop(
+            0,
+            chunks,
+            project,
+            (
+                jnp.zeros((ROWS, 1), jnp.float32),
+                jnp.zeros((ROWS, win.shape[1]), jnp.float32),
+            ),
         )
         inv = lax.rsqrt(total / width + EPSILON)
-
-        def project(k, acc):
-            h = stash[m, :, cols(k)].astype(jnp.float32)
-            n = (h * inv * gain_ref[:, cols(k)]).astype(jnp.bfloat16)
-            normed[m, :, cols(k)] = n
-            return acc + jnp.dot(
-                n, win[cols(k), :], preferred_element_type=jnp.float32
-            )
-
-        u = lax.fori_loop(
-            0, chunks, project, jnp.zeros((ROWS, win.shape[1]), jnp.float32)
-        )
+        u = u * inv
         act = (u * jax.nn.sigmoid(u)).astype(jnp.bfloat16)
         pre[m] = u
         scale[m] = jnp.broadcast_to(inv, scale.shape[1:])
-        act_out[m] = act
+        act_buf[m] = act
+
+        @pl.when(m == 0)
+        def _():
+            wout_copy.wait()
 
         @pl.when(not_last)
         def _():
@@ -163,6 +206,9 @@
 
             send_forward(m).start()
 
+        share(0, lambda owner: stash.at[m, :, part(owner)], all_h.at[me, m])
+        share(1, lambda owner: act_buf.at[m], all_act.at[me, m])
+
     def backward(m):
         pltpu.make_async_copy(up.at[m], up.at[m], b_recv.at[m]).wait()
 
@@ -177,8 +223,9 @@
         u = pre[m]
         inv = scale[m][:, :1]
         sig = jax.nn.sigmoid(u)
-        du = (da * sig * (1.0 + u * (1.0 - sig))).astype(jnp.bfloat16)
-        du_out[m] = du
+        wide_du = da * sig * (1.0 + u * (1.0 - sig))
+        du = wide_du.astype(jnp.bfloat16)
+        du_buf[m] = (wide_du * inv).astype(jnp.bfloat16)
         centered = jnp.sum(du.astype(jnp.float32) * u, axis=1, keepdims=True) / (
             inv * width
         )
@@ -189,7 +236,7 @@
             h = stash[m, :, cols(k)].astype(jnp.float32)
             dn = nt_dot(du, win[cols(k), :])
             rows = dn * h * inv
-            gg_out[:, cols(k)] += rows[:8] + rows[8:]
+            gain_acc[:, cols(k)] += rows[:8] + rows[8:]
 
             @pl.when(not_first)
             def _():
@@ -202,8 +249,8 @@
         def _():
             send_backward(m).start()
 
-        pltpu.make_async_copy(normed.at[m], n_out.at[m], o_sem.at[0, m]).start()
-        pltpu.make_async_copy(up.at[m], g_out.at[m], o_sem.at[1, m]).start()
+        share(2, lambda owner: up.at[m, :, part(owner)], all_g.at[me, m])
+        share(3, lambda owner: du_buf.at[m], all_du.at[me, m])
 
     @pl.loop(0, micros + 2 * DELAY * (sections - 1))
     def _(tick):
@@ -218,11 +265,10 @@
         def _():
             backward(mb)
 
+    share(4, lambda owner: gain_acc.at[:, part(owner)], all_gain.at[me])
+
     @pl.loop(0, micros)
     def _(m):
-        pltpu.make_async_copy(normed.at[m], n_out.at[m], o_sem.at[0, m]).wait()
-        pltpu.make_async_copy(up.at[m], g_out.at[m], o_sem.at[1, m]).wait()
-
         @pl.when(not_last)
         def _():
             send_forward(m).wait_send()
@@ -231,29 +277,35 @@
         def _():
             send_backward(m).wait_send()
 
-
-def local(sections, inputs, cotangent, weight_in, weight_out, norm_gains):
+    for kind, ref in enumerate((all_h, all_act, all_g, all_du, all_gain)):
+        sent = ref.at[pl.ds(0, replicas - 1)]
+        pltpu.make_async_copy(sent, sent, x_send.at[kind]).wait()
+        pltpu.make_async_copy(ref, ref, x_recv.at[kind]).wait()
+
+
+def local(sections, replicas, inputs, cotangent, weight_in, weight_out, norm_gains):
     tokens, width = inputs.shape
     hidden = weight_in.shape[2]
     micros = tokens // ROWS
-    wide = jax.ShapeDtypeStruct((micros, ROWS, width), jnp.bfloat16)
-    narrow = jax.ShapeDtypeStruct((micros, ROWS, hidden), jnp.bfloat16)
+    block = width // replicas
+    wide = jax.ShapeDtypeStruct((replicas, micros, ROWS, block), jnp.bfloat16)
+    narrow = jax.ShapeDtypeStruct((replicas, micros, ROWS, hidden), jnp.bfloat16)
     any_spec = pl.BlockSpec(memory_space=pl.ANY)
     vmem_spec = pl.BlockSpec(memory_space=pltpu.VMEM)
     wide_scratch = pltpu.VMEM((micros, ROWS, width), jnp.bfloat16)
     weight_scratch = pltpu.VMEM((width, hidden), jnp.bfloat16)
     dma = pltpu.SemaphoreType.DMA
-    all_norm, all_up, all_act, all_pre, gain_acc = pl.pallas_call(
-        functools.partial(relay_kernel, sections, micros),
+    all_h, all_g, all_act, all_du, all_gain = pl.pallas_call(
+        functools.partial(relay_kernel, sections, replicas, micros),
         out_shape=(
             wide,
             wide,
             narrow,
             narrow,
-            jax.ShapeDtypeStruct((8, width), jnp.float32),
+            jax.ShapeDtypeStruct((replicas, 8, block), jnp.float32),
         ),
         in_specs=[any_spec] * 4 + [vmem_spec],
-        out_specs=(any_spec, any_spec, vmem_spec, vmem_spec, vmem_spec),
+        out_specs=(any_spec,) * 5,
         scratch_shapes=[
             weight_scratch,
             weight_scratch,
@@ -261,7 +313,9 @@
             wide_scratch,
             wide_scratch,
             wide_scratch,
-            wide_scratch,
+            pltpu.VMEM((micros, ROWS, hidden), jnp.bfloat16),
+            pltpu.VMEM((micros, ROWS, hidden), jnp.bfloat16),
+            pltpu.VMEM((8, width), jnp.float32),
             pltpu.VMEM((micros, ROWS, hidden), jnp.float32),
             pltpu.VMEM((micros, ROWS, 128), jnp.float32),
             dma((2,)),
@@ -269,7 +323,8 @@
             dma((micros,)),
             dma((micros,)),
             dma((micros,)),
-            dma((2, micros)),
+            dma((5,)),
+            dma((5,)),
         ],
         compiler_params=pltpu.CompilerParams(
             collective_id=0, has_side_effects=True, vmem_limit_bytes=60 * 2**20
@@ -281,27 +336,23 @@
         weight_out[0],
         norm_gains,
     )
-    all_norm = all_norm.reshape(tokens, width)
-    all_up = all_up.reshape(tokens, width)
-    all_act = all_act.reshape(tokens, hidden)
-    all_pre = all_pre.reshape(tokens, hidden)
-    both_grads = lax.psum_scatter(
-        jnp.concatenate(
-            [column_product(all_norm, all_pre), column_product(all_up, all_act)], axis=1
-        ).astype(jnp.bfloat16),
-        "dp",
-        scatter_dimension=0,
-        tiled=True,
-    ).astype(jnp.float32)
-    gain_grad = lax.psum_scatter(
-        jnp.sum(gain_acc, axis=0).astype(jnp.bfloat16), "dp", scatter_dimension=0, tiled=True
-    ).astype(jnp.float32)
-    return (both_grads[:, :hidden][None], both_grads[:, hidden:][None], gain_grad[None])
+    total = replicas * tokens
+    own_gain = lax.dynamic_slice_in_dim(
+        norm_gains[0], lax.axis_index("dp") * block, block, 0
+    )
+    in_grad = own_gain[:, None] * column_product(
+        all_h.reshape(total, block), all_du.reshape(total, hidden)
+    )
+    out_grad = column_product(
+        all_g.reshape(total, block), all_act.reshape(total, hidden)
+    )
+    gain_grad = jnp.sum(all_gain, axis=(0, 1))
+    return (in_grad[None], out_grad[None], gain_grad[None])
 
 
 def solution(mesh):
     return jax.shard_map(
-        functools.partial(local, mesh.shape["section"]),
+        functools.partial(local, mesh.shape["section"], mesh.shape["dp"]),
         mesh=mesh,
         in_specs=(
             P("dp", None),

time: 308 us -> 171 us (0.56)
  waiting for transfers between devices: 89.2 us -> 0 us
  blocking collectives: 22.3 us -> 0 us
  between operations: 14.8 us -> 0.66 us
  other arithmetic: 9.84 us -> 0.62 us
  local copies, waits for them, and re-layouts: 7.68 us -> 0.7 us
    reduce_scatter x1 -> x0, waiting for transfers between devices: 89.2 us -> none  [local(): lax.psum_scatter(jnp.concatenate([column_product(all_norm, all_pre), colu...]
    unnamed x1 -> x0, blocking collectives: 22.3 us -> none
    concatenate x1 -> x0, other arithmetic: 7.14 us -> none  [local(): jnp.concatenate([column_product(all_norm, all_pre), column_product(all_up...]
    unnamed x11 -> x4, local copies, waits for them, and re-layouts: 5.9 us -> 0.01 us
  transfers between devices with their start and end apart: 1 -> 0, of which waited for: 1 -> 0; matrix products, arithmetic and copies ran while one was open for 0% -> 0% of each run, Pallas kernels for 0% -> 0%
where the time goes in v2:
time: 171 us; the launch traced here: 170 us
  Pallas kernels  159 us (93%)
  matrix products  9.32 us (5%)
    pallas_call x1, Pallas kernels, local(): pl.pallas_call(functools.partial(relay_kernel, sections, replicas, micros...  159 us
    dot_general x2, matrix products, column_product(): lax.dot_general(left, right, (((0,), (0,)), ((), ())), preferred_element_...  9.32 us

profile of v2, /device:TPU:0, one launch (start us, length us, event | category | flops | bytes accessed | tf_op | source)
XLA Modules:
  0.0 170.4 jit_solution(6045219992845636126)
XLA Ops:
  0.6 0.7 constant_dynamic-slice_fusion
  1.3 159.1 %shard_map.76 = (bf16[8,10,16,1024]{3,2,1,0:T(8,128)(2,1)}, bf16[8,10,16,1024]{3,2,1,0:T(8,128)(2,1)}, bf16[8,10,16,512]{3,2,1,0:T(8,128)(2,1)}, bf16[8,10,16,512]{3,2,1,0:T(8,128)(2,1)}, f32[8,8,1024]{2,1,0:T(8,128)}) custom-call(bf16[10,16,8192]{2,1,0:T(8,128)(2,1)} %bitcast.26, bf16[10,16,8192]{2,1,0:T(8,128)(2,1)} %bitcast.27, ...), custom_call_target="tpu_custom_call" | custom-call | tf_op jit(solution)/shard_map/pallas_call | solution.py:298
  160.4 0.0 copy-start
  160.4 0.0 copy-start.1
  160.4 5.1 %fusion = f32[1,1024,512]{2,1,0:T(8,128)} fusion(bf16[8,10,16,1024]{3,2,1,0:T(8,128)(2,1)} %get-tuple-element.8, bf16[8,10,16,512]{3,2,1,0:T(8,128)(2,1)} %get-tuple-element.9, f32[1024]{0:T(1024)S(1)} %bitcast.29), kind=kOutput, calls=%fused_computation.1 | convolution fusion | flops 1342701568 | bytes 6033408 | tf_op jit(solution)/shard_map/dot_general | solution.py:24
  165.6 0.0 copy-done
  165.6 0.6 reduce_sum.9
  166.2 0.0 copy-done.1
  166.2 4.2 %convolution_bitcast_fusion = f32[1,1024,512]{2,1,0:T(8,128)} fusion(bf16[8,10,16,1024]{3,2,1,0:T(8,128)(2,1)S(1)} %copy-done.1, bf16[8,10,16,512]{3,2,1,0:T(8,128)(2,1)} %get-tuple-element.11), kind=kOutput, calls=%fused_computation.2 | convolution fusion | flops 1342177280 | bytes 6029312 | tf_op jit(solution)/shard_map/dot_general | solution.py:24
Async XLA Ops:
  160.4 5.2 %copy-start = (f32[8,8,1024]{2,1,0:T(8,128)S(1)}, f32[8,8,1024]{2,1,0:T(8,128)}, u32[]{:S(2)}) copy-start(f32[8,8,1024]{2,1,0:T(8,128)} %get-tuple-element.12) | copy-start | bytes 786436
  160.4 5.8 %copy-start.1 = (bf16[8,10,16,1024]{3,2,1,0:T(8,128)(2,1)S(1)}, bf16[8,10,16,1024]{3,2,1,0:T(8,128)(2,1)}, u32[]{:S(2)}) copy-start(bf16[8,10,16,1024]{3,2,1,0:T(8,128)(2,1)} %get-tuple-element.10) | copy-start | bytes 7864324

commit v3 on v2

--- a/solution.py
+++ b/solution.py
@@ -8,8 +8,8 @@
 from jax.sharding import PartitionSpec as P
 
 ROWS = 16
-CHUNK = 2048
-DELAY = 2
+CHUNK = 4096
+DELAY = 1
 EPSILON = 1e-05
 MESH = pl.DeviceIdType.MESH
 
@@ -39,7 +39,6 @@
     all_g,
     all_act,
     all_du,
-    all_gain,
     win,
     wout,
     stash,
@@ -48,7 +47,6 @@
     out_b,
     act_buf,
     du_buf,
-    gain_acc,
     pre,
     scale,
     w_sem,
@@ -69,6 +67,9 @@
     not_first = pos > 0
     not_last = pos < sections - 1
 
+    def cols(k):
+        return pl.ds(pl.multiple_of(k * CHUNK, CHUNK), CHUNK)
+
     win_copy = pltpu.make_async_copy(win_hbm, win, w_sem.at[0])
     wout_copy = pltpu.make_async_copy(wout_hbm, wout, w_sem.at[1])
     win_copy.start()
@@ -77,7 +78,11 @@
     def _():
         @pl.loop(0, micros)
         def _(m):
-            pltpu.make_async_copy(x_ref.at[m], stash.at[m], f_recv.at[m]).start()
+            @pl.loop(0, chunks)
+            def _(k):
+                pltpu.make_async_copy(
+                    x_ref.at[m, :, cols(k)], stash.at[m, :, cols(k)], f_recv.at[m, k]
+                ).start()
 
     wout_copy.start()
 
@@ -85,7 +90,11 @@
     def _():
         @pl.loop(0, micros)
         def _(m):
-            pltpu.make_async_copy(c_ref.at[m], up.at[m], b_recv.at[m]).start()
+            @pl.loop(0, chunks)
+            def _(k):
+                pltpu.make_async_copy(
+                    c_ref.at[m, :, cols(k)], up.at[m, :, cols(k)], b_recv.at[m, k]
+                ).start()
 
     barrier = pltpu.get_barrier_semaphore()
 
@@ -115,27 +124,22 @@
         replicas - 1 + not_first.astype(jnp.int32) + not_last.astype(jnp.int32),
     )
 
-    gain_acc[...] = jnp.zeros_like(gain_acc)
-
-    def cols(k):
-        return pl.ds(pl.multiple_of(k * CHUNK, CHUNK), CHUNK)
-
-    def send_forward(m):
+    def send_forward(m, k):
         return pltpu.make_async_remote_copy(
-            src_ref=out_f.at[m],
-            dst_ref=stash.at[m],
-            send_sem=f_send.at[m],
-            recv_sem=f_recv.at[m],
+            src_ref=out_f.at[m, :, cols(k)],
+            dst_ref=stash.at[m, :, cols(k)],
+            send_sem=f_send.at[m, k],
+            recv_sem=f_recv.at[m, k],
             device_id={"section": pos + 1},
             device_id_type=MESH,
         )
 
-    def send_backward(m):
+    def send_backward(m, k):
         return pltpu.make_async_remote_copy(
-            src_ref=out_b.at[m],
-            dst_ref=up.at[m],
-            send_sem=b_send.at[m],
-            recv_sem=b_recv.at[m],
+            src_ref=out_b.at[m, :, cols(k)],
+            dst_ref=up.at[m, :, cols(k)],
+            send_sem=b_send.at[m, k],
+            recv_sem=b_recv.at[m, k],
             device_id={"section": pos - 1},
             device_id_type=MESH,
         )
@@ -159,14 +163,14 @@
         return pl.ds(pl.multiple_of(owner * block, block), block)
 
     def forward(m):
-        pltpu.make_async_copy(stash.at[m], stash.at[m], f_recv.at[m]).wait()
-
         @pl.when(m == 0)
         def _():
             win_copy.wait()
 
         def project(k, carry):
             total, acc = carry
+            piece = stash.at[m, :, cols(k)]
+            pltpu.make_async_copy(piece, piece, f_recv.at[m, k]).wait()
             h = stash[m, :, cols(k)].astype(jnp.float32)
             scaled = (h * gain_ref[:, cols(k)]).astype(jnp.bfloat16)
             return (
@@ -203,16 +207,15 @@
                 out_f[m, :, cols(k)] = (h + nt_dot(act, wout[cols(k), :])).astype(
                     jnp.bfloat16
                 )
-
-            send_forward(m).start()
+                send_forward(m, k).start()
 
         share(0, lambda owner: stash.at[m, :, part(owner)], all_h.at[me, m])
         share(1, lambda owner: act_buf.at[m], all_act.at[me, m])
 
     def backward(m):
-        pltpu.make_async_copy(up.at[m], up.at[m], b_recv.at[m]).wait()
-
         def project(k, acc):
+            piece = up.at[m, :, cols(k)]
+            pltpu.make_async_copy(piece, piece, b_recv.at[m, k]).wait()
             return acc + jnp.dot(
                 up[m, :, cols(k)], wout[cols(k), :], preferred_element_type=jnp.float32
             )
@@ -231,23 +234,17 @@
         )
         pull = inv * inv * inv * centered
 
-        @pl.loop(0, chunks)
-        def _(k):
-            h = stash[m, :, cols(k)].astype(jnp.float32)
-            dn = nt_dot(du, win[cols(k), :])
-            rows = dn * h * inv
-            gain_acc[:, cols(k)] += rows[:8] + rows[8:]
-
-            @pl.when(not_first)
-            def _():
+        @pl.when(not_first)
+        def _():
+            @pl.loop(0, chunks)
+            def _(k):
+                h = stash[m, :, cols(k)].astype(jnp.float32)
                 g = up[m, :, cols(k)].astype(jnp.float32)
+                dn = nt_dot(du, win[cols(k), :])
                 out_b[m, :, cols(k)] = (
                     g + inv * (dn * gain_ref[:, cols(k)]) - h * pull
                 ).astype(jnp.bfloat16)
-
-        @pl.when(not_first)
-        def _():
-            send_backward(m).start()
+                send_backward(m, k).start()
 
         share(2, lambda owner: up.at[m, :, part(owner)], all_g.at[me, m])
         share(3, lambda owner: du_buf.at[m], all_du.at[me, m])
@@ -265,19 +262,19 @@
         def _():
             backward(mb)
 
-    share(4, lambda owner: gain_acc.at[:, part(owner)], all_gain.at[me])
-
     @pl.loop(0, micros)
     def _(m):
-        @pl.when(not_last)
-        def _():
-            send_forward(m).wait_send()
-
-        @pl.when(not_first)
-        def _():
-            send_backward(m).wait_send()
-
-    for kind, ref in enumerate((all_h, all_act, all_g, all_du, all_gain)):
+        @pl.loop(0, chunks)
+        def _(k):
+            @pl.when(not_last)
+            def _():
+                send_forward(m, k).wait_send()
+
+            @pl.when(not_first)
+            def _():
+                send_backward(m, k).wait_send()
+
+    for kind, ref in enumerate((all_h, all_act, all_g, all_du)):
         sent = ref.at[pl.ds(0, replicas - 1)]
         pltpu.make_async_copy(sent, sent, x_send.at[kind]).wait()
         pltpu.make_async_copy(ref, ref, x_recv.at[kind]).wait()
@@ -295,17 +292,16 @@
     wide_scratch = pltpu.VMEM((micros, ROWS, width), jnp.bfloat16)
     weight_scratch = pltpu.VMEM((width, hidden), jnp.bfloat16)
     dma = pltpu.SemaphoreType.DMA
-    all_h, all_g, all_act, all_du, all_gain = pl.pallas_call(
+    all_h, all_g, all_act, all_du = pl.pallas_call(
         functools.partial(relay_kernel, sections, replicas, micros),
         out_shape=(
             wide,
             wide,
             narrow,
             narrow,
-            jax.ShapeDtypeStruct((replicas, 8, block), jnp.float32),
         ),
         in_specs=[any_spec] * 4 + [vmem_spec],
-        out_specs=(any_spec,) * 5,
+        out_specs=(any_spec,) * 4,
         scratch_shapes=[
             weight_scratch,
             weight_scratch,
@@ -315,16 +311,15 @@
             wide_scratch,
             pltpu.VMEM((micros, ROWS, hidden), jnp.bfloat16),
             pltpu.VMEM((micros, ROWS, hidden), jnp.bfloat16),
-            pltpu.VMEM((8, width), jnp.float32),
             pltpu.VMEM((micros, ROWS, hidden), jnp.float32),
             pltpu.VMEM((micros, ROWS, 128), jnp.float32),
             dma((2,)),
-            dma((micros,)),
-            dma((micros,)),
-            dma((micros,)),
-            dma((micros,)),
-            dma((5,)),
-            dma((5,)),
+            dma((micros, width // CHUNK)),
+            dma((micros, width // CHUNK)),
+            dma((micros, width // CHUNK)),
+            dma((micros, width // CHUNK)),
+            dma((4,)),
+            dma((4,)),
         ],
         compiler_params=pltpu.CompilerParams(
             collective_id=0, has_side_effects=True, vmem_limit_bytes=60 * 2**20
@@ -337,16 +332,17 @@
         norm_gains,
     )
     total = replicas * tokens
-    own_gain = lax.dynamic_slice_in_dim(
-        norm_gains[0], lax.axis_index("dp") * block, block, 0
-    )
-    in_grad = own_gain[:, None] * column_product(
+    own = lax.axis_index("dp") * block
+    own_gain = lax.dynamic_slice_in_dim(norm_gains[0], own, block, 0)
+    own_rows = lax.dynamic_slice_in_dim(weight_in[0], own, block, 0)
+    raw_grad = column_product(
         all_h.reshape(total, block), all_du.reshape(total, hidden)
     )
+    in_grad = own_gain[:, None] * raw_grad
+    gain_grad = jnp.sum(own_rows.astype(jnp.float32) * raw_grad, axis=1)
     out_grad = column_product(
         all_g.reshape(total, block), all_act.reshape(total, hidden)
     )
-    gain_grad = jnp.sum(all_gain, axis=(0, 1))
     return (in_grad[None], out_grad[None], gain_grad[None])
 
 

time: 171 us -> 148 us (0.87)
  Pallas kernels: 159 us -> 134 us
  local copies, waits for them, and re-layouts: 0.7 us -> 4.32 us
    pallas_call x1, Pallas kernels: 159 us -> 134 us  [local(): pl.pallas_call(functools.partial(relay_kernel, sections, replicas, micros...]
    unnamed x4 -> x2, local copies, waits for them, and re-layouts: 0.01 us -> 2.34 us
where the time goes in v3:
time: 148 us
  Pallas kernels  134 us (91%)
  matrix products  9.27 us (6%)
  local copies, waits for them, and re-layouts  4.32 us (3%)
    pallas_call x1, Pallas kernels, local(): pl.pallas_call(functools.partial(relay_kernel, sections, replicas, micros...  134 us
    dot_general x2, matrix products, column_product(): lax.dot_general(left, right, (((0,), (0,)), ((), ())), preferred_element_...  9.27 us

profile of v3, /device:TPU:0, one launch (start us, length us, event | category | flops | bytes accessed | tf_op | source)
XLA Modules:
  0.0 148.0 jit_solution(9051774470019323773)
XLA Ops:
  0.6 0.7 constant_dynamic-slice_fusion.1
  1.3 1.3 constant_dynamic-slice_fusion
  2.6 0.5 copy.12
  3.2 133.8 %shard_map.76 = (bf16[8,10,16,1024]{3,2,1,0:T(8,128)(2,1)}, bf16[8,10,16,1024]{3,2,1,0:T(8,128)(2,1)}, bf16[8,10,16,512]{3,2,1,0:T(8,128)(2,1)}, bf16[8,10,16,512]{3,2,1,0:T(8,128)(2,1)}) custom-call(bf16[10,16,8192]{2,1,0:T(8,128)(2,1)} %bitcast.30, bf16[10,16,8192]{2,1,0:T(8,128)(2,1)} %bitcast.31, bf16[8192,512]{1,0:T(8,128)(2,1)} %bitcast.28, ...), custom_call_target="tpu_custom_call" | custom-call | tf_op jit(solution)/shard_map/pallas_call | solution.py:295
  137.0 4.3 %fusion = (f32[1024]{0:T(1024)}, f32[1,1024,512]{1,2,0:T(8,128)S(1)}) fusion(bf16[1,1024,512]{1,2,0:T(8,128)(2,1)S(1)} %copy.12, f32[1024]{0:T(1024)S(1)} %bitcast.32, bf16[8,10,16,1024]{3,2,1,0:T(8,128)(2,1)} %get-tuple-element.7, bf16[8,10,16,512]{3,2,1,0:T(8,128)(2,1)} %get-tuple-element.8), kind=kOutput, calls=%fused_computation.1 | convolution fusion | flops 1344273408 | bytes 7086080 | tf_op jit(solution)/shard_map/dot_general | solution.py:24
  141.3 1.8 %copy.9 = f32[1,1024,512]{2,1,0:T(8,128)} copy(f32[1,1024,512]{1,2,0:T(8,128)S(1)} %get-tuple-element.15) | data formatting | bytes 4194304
  143.1 5.0 %convolution_bitcast_fusion = f32[1,1024,512]{2,1,0:T(8,128)} fusion(bf16[8,10,16,1024]{3,2,1,0:T(8,128)(2,1)} %get-tuple-element.9, bf16[8,10,16,512]{3,2,1,0:T(8,128)(2,1)} %get-tuple-element.10), kind=kOutput, calls=%fused_computation.4 | convolution fusion | flops 1342177280 | bytes 6029312 | tf_op jit(solution)/shard_map/dot_general | solution.py:24

commit v4 on v3

--- a/solution.py
+++ b/solution.py
@@ -39,6 +39,8 @@
     all_g,
     all_act,
     all_du,
+    own_rows,
+    own_gain,
     win,
     wout,
     stash,
@@ -70,9 +72,12 @@
     def cols(k):
         return pl.ds(pl.multiple_of(k * CHUNK, CHUNK), CHUNK)
 
-    win_copy = pltpu.make_async_copy(win_hbm, win, w_sem.at[0])
-    wout_copy = pltpu.make_async_copy(wout_hbm, wout, w_sem.at[1])
-    win_copy.start()
+    def load_in(k):
+        return pltpu.make_async_copy(
+            win_hbm.at[cols(k), :], win.at[cols(k), :], w_sem.at[k]
+        )
+
+    wout_copy = pltpu.make_async_copy(wout_hbm, wout, w_sem.at[chunks])
 
     @pl.when(is_first)
     def _():
@@ -83,6 +88,10 @@
                 pltpu.make_async_copy(
                     x_ref.at[m, :, cols(k)], stash.at[m, :, cols(k)], f_recv.at[m, k]
                 ).start()
+
+    @pl.loop(0, chunks)
+    def _(k):
+        load_in(k).start()
 
     wout_copy.start()
 
@@ -163,12 +172,12 @@
         return pl.ds(pl.multiple_of(owner * block, block), block)
 
     def forward(m):
-        @pl.when(m == 0)
-        def _():
-            win_copy.wait()
-
         def project(k, carry):
             total, acc = carry
+            @pl.when(m == 0)
+            def _():
+                load_in(k).wait()
+
             piece = stash.at[m, :, cols(k)]
             pltpu.make_async_copy(piece, piece, f_recv.at[m, k]).wait()
             h = stash[m, :, cols(k)].astype(jnp.float32)
@@ -262,6 +271,13 @@
         def _():
             backward(mb)
 
+    own_copies = (
+        pltpu.make_async_copy(win.at[part(me), :], own_rows, w_sem.at[0]),
+        pltpu.make_async_copy(gain_ref.at[:, part(me)], own_gain, w_sem.at[1]),
+    )
+    own_copies[0].start()
+    own_copies[1].start()
+
     @pl.loop(0, micros)
     def _(m):
         @pl.loop(0, chunks)
@@ -274,6 +290,8 @@
             def _():
                 send_backward(m, k).wait_send()
 
+    own_copies[0].wait()
+    own_copies[1].wait()
     for kind, ref in enumerate((all_h, all_act, all_g, all_du)):
         sent = ref.at[pl.ds(0, replicas - 1)]
         pltpu.make_async_copy(sent, sent, x_send.at[kind]).wait()
@@ -292,16 +310,18 @@
     wide_scratch = pltpu.VMEM((micros, ROWS, width), jnp.bfloat16)
     weight_scratch = pltpu.VMEM((width, hidden), jnp.bfloat16)
     dma = pltpu.SemaphoreType.DMA
-    all_h, all_g, all_act, all_du = pl.pallas_call(
+    all_h, all_g, all_act, all_du, own_rows, own_gain = pl.pallas_call(
         functools.partial(relay_kernel, sections, replicas, micros),
         out_shape=(
             wide,
             wide,
             narrow,
             narrow,
+            jax.ShapeDtypeStruct((block, hidden), jnp.bfloat16),
+            jax.ShapeDtypeStruct((1, block), jnp.float32),
         ),
         in_specs=[any_spec] * 4 + [vmem_spec],
-        out_specs=(any_spec,) * 4,
+        out_specs=(any_spec,) * 6,
         scratch_shapes=[
             weight_scratch,
             weight_scratch,
@@ -313,7 +333,7 @@
             pltpu.VMEM((micros, ROWS, hidden), jnp.bfloat16),
             pltpu.VMEM((micros, ROWS, hidden), jnp.float32),
             pltpu.VMEM((micros, ROWS, 128), jnp.float32),
-            dma((2,)),
+            dma((width // CHUNK + 2,)),
             dma((micros, width // CHUNK)),
             dma((micros, width // CHUNK)),
             dma((micros, width // CHUNK)),
@@ -332,13 +352,10 @@
         norm_gains,
     )
     total = replicas * tokens
-    own = lax.axis_index("dp") * block
-    own_gain = lax.dynamic_slice_in_dim(norm_gains[0], own, block, 0)
-    own_rows = lax.dynamic_slice_in_dim(weight_in[0], own, block, 0)
     raw_grad = column_product(
         all_h.reshape(total, block), all_du.reshape(total, hidden)
     )
-    in_grad = own_gain[:, None] * raw_grad
+    in_grad = own_gain[0][:, None] * raw_grad
     gain_grad = jnp.sum(own_rows.astype(jnp.float32) * raw_grad, axis=1)
     out_grad = column_product(
         all_g.reshape(total, block), all_act.reshape(total, hidden)

time: 148 us -> 152 us (1.027)
  other arithmetic: 0 us -> 4 us
    reduce_sum x0 -> x1, other arithmetic: none -> 2.46 us  [local(): gain_grad = jnp.sum(own_rows.astype(jnp.float32) * raw_grad, axis=1)]
    dynamic_slice x2 -> x0, local copies, waits for them, and re-layouts: 1.98 us -> none  [the longest x1 1.29 us: local(): own_rows = lax.dynamic_slice_in_dim(weight_in[0], own, block, 0)]
    dot_general x0 -> x1, local copies, waits for them, and re-layouts: none -> 1.81 us  [column_product(): lax.dot_general(left, right, (((0,), (0,)), ((), ())), preferred_element_...]
    broadcast_in_dim x0 -> x1, other arithmetic: none -> 1.54 us  [local(): return (in_grad[None], out_grad[None], gain_grad[None])]
    unnamed x2 -> x7, local copies, waits for them, and re-layouts: 2.34 us -> 3.04 us
where the time goes in v4:
time: 152 us; the launch traced here: 151 us
  Pallas kernels  134 us (88%)
  matrix products  7.84 us (5%)
  local copies, waits for them, and re-layouts  4.86 us (3%)
  other arithmetic  4 us (3%)
    pallas_call x1, Pallas kernels, local(): pl.pallas_call(functools.partial(relay_kernel, sections, replicas, micros...  134 us
    dot_general x2, matrix products, column_product(): lax.dot_general(left, right, (((0,), (0,)), ((), ())), preferred_element_...  7.84 us
    unnamed x7, local copies, waits for them, and re-layouts  3.04 us

profile of v4, /device:TPU:0, one launch (start us, length us, event | category | flops | bytes accessed | tf_op | source)
XLA Modules:
  0.0 151.3 jit_solution(13701689466985136529)
XLA Ops:
  0.6 134.0 %shard_map.76 = (bf16[8,10,16,1024]{3,2,1,0:T(8,128)(2,1)}, bf16[8,10,16,1024]{3,2,1,0:T(8,128)(2,1)}, bf16[8,10,16,512]{3,2,1,0:T(8,128)(2,1)}, bf16[8,10,16,51...) custom-call(bf16[10,16,8192]{2,1,0:T(8,128)(2,1)} %bitcast.24, bf16[10,16,8192]{2,1,0:T(8,128)(2,1)} %bitcast.25, ...), custom_call_target="tpu_custom_call" | custom-call | tf_op jit(solution)/shard_map/pallas_call | solution.py:313
  134.6 3.7 %convolution_bitcast_fusion.1 = f32[1024,512]{0,1:T(8,128)S(1)} fusion(bf16[8,10,16,1024]{3,2,1,0:T(8,128)(2,1)} %get-tuple-element.10, bf16[8,10,16,512]{3,2,1,0:T(8,128)(2,1)} %get-tuple-element.11), kind=kOutput, calls=%fused_computation.3 | convolution fusion | flops 1342177280 | bytes 6029312 | tf_op jit(solution)/shard_map/dot_general | solution.py:24
  138.3 0.0 copy-start
  138.3 1.8 %copy.8 = f32[1024,512]{1,0:T(8,128)} copy(f32[1024,512]{0,1:T(8,128)S(1)} %convolution_bitcast_fusion.1) | data formatting | bytes 4194304 | tf_op jit(solution)/shard_map/dot_general | solution.py:24
  140.1 0.0 copy-start.1
  140.1 0.0 copy-done
  140.1 2.5 %multiply_reduce_fusion = f32[1024]{0:T(1024)} fusion(f32[1024,512]{1,0:T(8,128)} %copy.8, bf16[1024,512]{1,0:T(8,128)(2,1)S(1)} %copy-done), kind=kLoop, calls=%fused_computation | loop fusion | flops 1571840 | bytes 3149824 | tf_op jit(solution)/shard_map/reduce_sum | solution.py:359
  142.6 0.0 copy-done.1
  142.6 1.5 %multiply_bitcast_fusion = f32[1,1024,512]{1,2,0:T(8,128)} fusion(f32[1024,512]{0,1:T(8,128)S(1)} %convolution_bitcast_fusion.1, f32[1024]{0:T(1024)S(1)} %bitcast.27), kind=kLoop, calls=%fused_computation.1 | loop fusion | flops 524288 | bytes 4198400 | tf_op jit(solution)/shard_map/broadcast_in_dim | solution.py:363
  144.1 0.0 copy-start.2
  144.1 3.0 %copy.9 = f32[1,1024,512]{2,1,0:T(8,128)} copy(f32[1,1024,512]{1,2,0:T(8,128)} %multiply_bitcast_fusion) | data formatting | bytes 4194304
  147.1 0.0 copy-done.2
  147.1 4.2 %convolution_bitcast_fusion = f32[1,1024,512]{2,1,0:T(8,128)} fusion(bf16[8,10,16,1024]{3,2,1,0:T(8,128)(2,1)S(1)} %copy-done.2, bf16[8,10,16,512]{3,2,1,0:T(8,128)(2,1)} %get-tuple-element.13), kind=kOutput, calls=%fused_computation.2 | convolution fusion | flops 1342177280 | bytes 6029312 | tf_op jit(solution)/shard_map/dot_general | solution.py:24
Async XLA Ops:
  138.3 1.8 %copy-start = (bf16[1024,512]{1,0:T(8,128)(2,1)S(1)}, bf16[1024,512]{1,0:T(8,128)(2,1)}, u32[]{:S(2)}) copy-start(bf16[1024,512]{1,0:T(8,128)(2,1)} %get-tuple-element.14) | copy-start | bytes 3145732
  140.1 2.5 %copy-start.1 = (f32[1,1024]{1,0:T(1,128)S(1)}, f32[1,1024]{1,0:T(1,128)}, u32[]{:S(2)}) copy-start(f32[1,1024]{1,0:T(1,128)} %get-tuple-element.9) | copy-start | bytes 12292
  144.1 3.0 %copy-start.2 = (bf16[8,10,16,1024]{3,2,1,0:T(8,128)(2,1)S(1)}, bf16[8,10,16,1024]{3,2,1,0:T(8,128)(2,1)}, u32[]{:S(2)}) copy-start(bf16[8,10,16,1024]{3,2,1,0:T(8,128)(2,1)} %get-tuple-element.12) | copy-start | bytes 7864324
